TPU v7x, 256 devices: a whole 4x4x8 slice. The times are simulated.
256 devices in a mesh: grp: 8 (over x, z_lo), dev: 32 (over y, z_hi, core).
Axes of the slice: x: 4, y: 4, z: 8 (z_hi: 4, z_lo: 2; z = z_hi * 2 + z_lo), core: 2. Of those that a mesh axis runs over, the one named last changes fastest.
Arguments:
- query: bfloat16 [512, 128, 4096], P(('grp', 'dev')), may hold values from -100 to 100
- grad_out: bfloat16 [512, 128, 4096], P(('grp', 'dev')), may hold values from -6 to 6
- branch_kv: bfloat16 [512, 128, 1024], P(('grp', 'dev')), may hold values from -6 to 6
- root_kv: bfloat16 [1024, 1024], P('dev'), may hold values from -24 to 24
- lengths: int32 [512], P(('grp', 'dev')), may hold values from 0 to 128, as said below
- segments: int32 [512], P(('grp', 'dev')), may hold values from 0 to 3
Outputs:
- query_grad: bfloat16 [512, 128, 4096], P(('grp', 'dev'))
- branch_grad: bfloat16 [512, 128, 1024], P(('grp', 'dev'))
- root_grad: float32 [1024, 1024], P('dev')
Inputs may be any that keep to these rules, and one draw needn't show every extreme that they name: `lengths`: A slot with length 0 holds no branch. A device's slots with live positions come before its empty slots. Within a group, device d and device d + 32/2 (d < 16) hold exactly 2 slots with live positions together; a quarter of a group's devices hold 2 such slots and a quarter hold none.
All inputs are finite; a program needn't handle non-finite values.
Results may differ from a plain program's by a relative error of at most 0.0069.
Values may be sent and summed in bfloat16 or wider, within the bound.
A program may use at most 128 MiB of HBM per device.

v0:
```python
import jax
import jax.numpy as jnp
from jax import lax
from jax.sharding import PartitionSpec as P

H = 32
KVH = 4
DH = 128
SEGS = 4


def passed_along(block, axis, distance):
    devices = range(lax.axis_size(axis))
    route = [((i - distance) % len(devices), i) for i in devices]
    return lax.ppermute(block, axis, route)


def cut_along(x, dim, peers):
    dims = x.shape
    blocks = x.reshape(*dims[:dim], peers, dims[dim] // peers, *dims[dim + 1 :])
    return jnp.moveaxis(blocks, dim, 0)


def summed_on_arrival(x, axis, dim):
    blocks = cut_along(x, dim, lax.axis_size(axis))
    arrived = lax.all_to_all(blocks, axis, split_axis=0, concat_axis=0, tiled=True)
    return arrived.astype(jnp.float32).sum(axis=0)


def from_everyone(x, axis):
    copies = jnp.broadcast_to(x, (lax.axis_size(axis), *x.shape))
    return lax.all_to_all(copies, axis, split_axis=0, concat_axis=0, tiled=True)


def over_copies(x, axis):
    return from_everyone(x, axis).sum(axis=0)


def tile_grads(query, grad, branch, length, segment, root_keys):
    rows = query.shape[0]
    width = KVH * DH
    groups = H // KVH
    roots = root_keys.shape[0]
    everything = jnp.concatenate([root_keys, branch], axis=0)
    span = roots + rows
    scale = DH ** (-0.5)
    row_pos = lax.broadcasted_iota(jnp.int32, (rows, span), 0)
    col_pos = lax.broadcasted_iota(jnp.int32, (rows, span), 1)
    visible = jnp.where(
        col_pos < roots, col_pos < (segment + 1) * (roots // SEGS), col_pos - roots <= row_pos
    )
    live = lax.broadcasted_iota(jnp.int32, (rows, 1), 0) < length
    grad = jnp.where(live, grad, jnp.zeros_like(grad))
    dq_parts = []
    dk_parts = []
    dv_parts = []
    for head in range(KVH):
        q_head = query[:, head * groups * DH : (head + 1) * groups * DH].reshape(rows, groups, DH)
        g_head = grad[:, head * groups * DH : (head + 1) * groups * DH].reshape(rows, groups, DH)
        k_head = everything[:, head * DH : (head + 1) * DH]
        v_head = everything[:, width + head * DH : width + (head + 1) * DH]
        scores = (
            jnp.einsum("tgd,ld->gtl", q_head, k_head, preferred_element_type=jnp.float32) * scale
        )
        scores = jnp.where(visible[None], scores, jnp.float32(-1e30))
        peak = jnp.max(scores, axis=-1, keepdims=True)
        weights = jnp.exp(scores - peak)
        weights = weights / jnp.sum(weights, axis=-1, keepdims=True)
        probs = weights.astype(jnp.bfloat16)
        output = jnp.einsum("gtl,ld->tgd", probs, v_head, preferred_element_type=jnp.float32)
        delta = jnp.sum(g_head.astype(jnp.float32) * output, axis=-1)
        dv_parts.append(
            jnp.einsum("gtl,tgd->ld", probs, g_head, preferred_element_type=jnp.float32)
        )
        prob_grad = jnp.einsum("tgd,ld->gtl", g_head, v_head, preferred_element_type=jnp.float32)
        score_grad = (weights * (prob_grad - delta.T[:, :, None]) * scale).astype(jnp.bfloat16)
        dq_parts.append(
            jnp.einsum(
                "gtl,ld->tgd", score_grad, k_head, preferred_element_type=jnp.float32
            ).reshape(rows, groups * DH)
        )
        dk_parts.append(
            jnp.einsum("gtl,tgd->ld", score_grad, q_head, preferred_element_type=jnp.float32)
        )
    dq = jnp.concatenate(dq_parts, axis=1).astype(jnp.bfloat16)
    dkv = jnp.concatenate(dk_parts + dv_parts, axis=1)
    return (dq, dkv[roots:].astype(jnp.bfloat16), dkv[:roots])


def local(query, grad_out, branch_kv, root_kv, lengths, segments):
    root_keys = lax.all_gather(root_kv, "dev", axis=0, tiled=True)
    half = lax.axis_size("dev") // 2
    live_count = jnp.sum((lengths > 0).astype(jnp.int32))
    arrived = passed_along(
        (query[1], grad_out[1], branch_kv[1], lengths[1:], segments[1:]), "dev", half
    )
    resident = live_count > 0
    q_tile = jnp.where(resident, query[0], arrived[0])
    g_tile = jnp.where(resident, grad_out[0], arrived[1])
    b_tile = jnp.where(resident, branch_kv[0], arrived[2])
    length = jnp.where(resident, lengths[0], arrived[3][0])
    segment = jnp.where(resident, segments[0], arrived[4][0])
    dq, dbranch, total = tile_grads(q_tile, g_tile, b_tile, length, segment, root_keys)
    returned = passed_along((dq, dbranch), "dev", half)
    second = live_count > 1
    query_grad = jnp.stack(
        [
            jnp.where(resident, dq, jnp.zeros_like(dq)),
            jnp.where(second, returned[0], jnp.zeros_like(dq)),
        ]
    )
    branch_grad = jnp.stack(
        [
            jnp.where(resident, dbranch, jnp.zeros_like(dbranch)),
            jnp.where(second, returned[1], jnp.zeros_like(dbranch)),
        ]
    )
    within = summed_on_arrival(total.astype(jnp.bfloat16), "dev", 0)
    root_grad = over_copies(within, "grp")
    return (query_grad, branch_grad, root_grad)


def solution(mesh):
    placed = (
        P(("grp", "dev"), None, None),
        P(("grp", "dev"), None, None),
        P(("grp", "dev"), None, None),
        P("dev", None),
        P(("grp", "dev")),
        P(("grp", "dev")),
    )
    return jax.shard_map(
        local,
        mesh=mesh,
        in_specs=placed,
        out_specs=(P(("grp", "dev"), None, None), P(("grp", "dev"), None, None), P("dev", None)),
        check_vma=False,
    )
```

profile of v0, /device:TPU:8, one launch (start us, length us, event | category | flops | bytes accessed | tf_op | source)
XLA Modules:
  0.0 251.1 jit_solution(15265945719861936562)
XLA Ops:
  8.2 2.4 collective-permute-start
  10.6 1.3 fusion.109
  11.9 1.2 collective-permute-start.1
  13.1 1.7 fusion.105
  14.8 1.3 copy.208
  16.2 2.3 collective-permute-start.2
  19.0 1.2 collective-permute-start.3
  20.3 1.7 fusion.106
  22.0 1.3 copy.210
  23.3 2.3 collective-permute-start.4
  29.4 1.2 fusion.45
  30.7 14.4 %collective-permute-done.3 = s32[1]{0:T(128)} collective-permute-done((s32[1]{0:T(128)}, s32[1]{0:T(128)}, u32[]{:S(2)}, u32[]{:S(2)}) %collective-permute-start.3) | collective-permute-done | bytes 36 | tf_op jit(solution)/shard_map/ppermute | solution.py:15
  46.4 1.0 bitcast_select_fusion.10
  48.5 17.4 %collective-permute-done.4 = bf16[128,4096]{0,1:T(8,128)(2,1)} collective-permute-done((bf16[128,4096]{0,1:T(8,128)(2,1)}, bf16[128,4096]{0,1:T(8,128)(2,1)}, u32[]{:S(2)}, u32[]{:S(2)}) %collective-permute-start.4) | collective-permute-done | bytes 1048608 | tf_op jit(solution)/shard_map/ppermute | solution.py:15
  67.7 29.8 %all-gather.2.cloned.1.call-done = bf16[1024,1024]{1,0:T(8,128)(2,1)} async-done(((bf16[32,1024]{1,0:T(8,128)(2,1)}), bf16[1024,1024]{1,0:T(8,128)(2,1)}) %all-gather.2.cloned.1.call-update) | async-done | bytes 2097168 | tf_op jit(solution)/shard_map/all_gather | solution.py:91
  97.5 2.3 fusion.47
  99.8 4.4 %exponential_reduce_fusion.3 = (f32[8,128]{1,0:T(8,128)}, f32[8,128,1152]{1,2,0:T(8,128)}) fusion(pred[128,1152]{0,1:T(8,128)(4,1)S(1)} %fusion.45, bf16[128,8,128]{0,2,1:T(8,128)(2,1)S(1)} %bitcast.302, bf16[1152,128]{1,0:T(8,128)(2,1)S(1)} %get-tuple-element.11), kind=kOutput, calls=%fused_computation.50 | convolution fusion | flops 306709632 | bytes 5427200 | tf_op jit(solution)/shard_map/sub | solution.py:67
  104.2 3.1 %fusion.40 = bf16[8,128,1152]{1,2,0:T(8,128)(2,1)S(1)} fusion(f32[8,128]{1,0:T(8,128)} %get-tuple-element.38, f32[8,128,1152]{1,2,0:T(8,128)} %get-tuple-element.39), kind=kLoop, calls=%fused_computation.77 | loop fusion | flops 2359296 | bytes 7081984 | tf_op jit(solution)/shard_map/convert_element_type | solution.py:69
  107.9 1.8 copy-done.20
  109.7 1.3 fusion.19
  111.0 1.6 fusion.31
  112.6 5.4 %exponential_reduce_fusion.2 = (f32[8,128]{1,0:T(8,128)}, f32[8,128,1152]{1,2,0:T(8,128)}) fusion(pred[128,1152]{0,1:T(8,128)(4,1)S(1)} %fusion.45, bf16[128,8,128]{0,2,1:T(8,128)(2,1)} %bitcast.300, bf16[1152,128]{1,0:T(8,128)(2,1)} %get-tuple-element.12), kind=kOutput, calls=%fused_computation.48 | convolution fusion | flops 306709632 | bytes 5427200 | tf_op jit(solution)/shard_map/sub | solution.py:67
  118.0 3.1 %fusion.41 = bf16[8,128,1152]{1,2,0:T(8,128)(2,1)S(1)} fusion(f32[8,128]{1,0:T(8,128)} %get-tuple-element.36, f32[8,128,1152]{1,2,0:T(8,128)} %get-tuple-element.37), kind=kLoop, calls=%fused_computation.78 | loop fusion | flops 2359296 | bytes 7081984 | tf_op jit(solution)/shard_map/convert_element_type | solution.py:69
  122.6 1.7 copy-done.21
  124.4 1.3 fusion.16
  125.7 1.5 fusion.30
  127.3 5.4 %exponential_reduce_fusion.1 = (f32[8,128]{1,0:T(8,128)}, f32[8,128,1152]{1,2,0:T(8,128)}) fusion(pred[128,1152]{0,1:T(8,128)(4,1)S(1)} %fusion.45, bf16[128,8,128]{0,2,1:T(8,128)(2,1)} %bitcast.298, bf16[1152,128]{1,0:T(8,128)(2,1)} %get-tuple-element.13), kind=kOutput, calls=%fused_computation.46 | convolution fusion | flops 306709632 | bytes 5427200 | tf_op jit(solution)/shard_map/sub | solution.py:67
  132.7 3.3 %fusion.42 = bf16[8,128,1152]{1,2,0:T(8,128)(2,1)S(1)} fusion(f32[8,128]{1,0:T(8,128)} %get-tuple-element.34, f32[8,128,1152]{1,2,0:T(8,128)} %get-tuple-element.35), kind=kLoop, calls=%fused_computation.79 | loop fusion | flops 2359296 | bytes 7081984 | tf_op jit(solution)/shard_map/convert_element_type | solution.py:69
  137.4 1.8 copy-done.19
  139.2 1.3 fusion.13
  140.6 1.6 fusion.29
  142.2 5.3 %exponential_reduce_fusion = (f32[8,128]{1,0:T(8,128)}, f32[8,128,1152]{1,2,0:T(8,128)}) fusion(pred[128,1152]{0,1:T(8,128)(4,1)S(1)} %fusion.45, bf16[128,8,128]{0,2,1:T(8,128)(2,1)S(1)} %bitcast.296, bf16[1152,128]{1,0:T(8,128)(2,1)} %get-tuple-element.15), kind=kOutput, calls=%fused_computation.44 | convolution fusion | flops 306709632 | bytes 5427200 | tf_op jit(solution)/shard_map/sub | solution.py:67
  147.5 3.1 %fusion.43 = bf16[8,128,1152]{1,2,0:T(8,128)(2,1)S(1)} fusion(f32[8,128]{1,0:T(8,128)} %get-tuple-element.32, f32[8,128,1152]{1,2,0:T(8,128)} %get-tuple-element.33), kind=kLoop, calls=%fused_computation.80 | loop fusion | flops 2359296 | bytes 7081984 | tf_op jit(solution)/shard_map/convert_element_type | solution.py:69
  150.7 1.5 multiply_reduce_fusion
  152.3 1.3 fusion.10
  160.5 1.6 slice.137
  162.6 7.3 %all-to-all-start = ((bf16[32,32,1024]{2,1,0:T(8,128)(2,1)}), bf16[32,32,1024]{2,1,0:T(8,128)(2,1)}, u32[]{:S(2)}, u32[]{:S(2)}) async-start(bf16[32,32,1024]{2,1,0:T(8,128)(2,1)} %bitcast.275), calls=%async_computation | async-start | bytes 4194304 | tf_op jit(solution)/shard_map/all_to_all | solution.py:26
  170.6 1.9 select_bitcast_fusion.2
  172.5 2.1 collective-permute-start.6
  174.6 1.5 convolution_convert_fusion.3
  178.4 1.1 pad_maximum_fusion.1
  179.5 1.4 collective-permute-start.5
  180.9 38.8 %all-to-all-done = bf16[32,32,1024]{2,1,0:T(8,128)(2,1)} async-done(((bf16[32,32,1024]{2,1,0:T(8,128)(2,1)}), bf16[32,32,1024]{2,1,0:T(8,128)(2,1)}, u32[]{:S(2)}, u32[]{:S(2)}) %all-to-all-start) | async-done | bytes 2097184 | tf_op jit(solution)/shard_map/all_to_all | solution.py:26
  219.7 2.0 convert_reduce_fusion
  221.6 1.1 broadcast_in_dim.54
  222.7 4.3 %all-to-all-start.1 = ((f32[8,32,1024]{2,1,0:T(8,128)}), f32[8,32,1024]{2,1,0:T(8,128)S(1)}, u32[]{:S(2)}, u32[]{:S(2)}) async-start(f32[8,32,1024]{2,1,0:T(8,128)} %broadcast_in_dim.54), calls=%async_computation.1 | async-start | bytes 2097152 | tf_op jit(solution)/shard_map/all_to_all | solution.py:32
  229.0 2.7 %copy.150 = bf16[2,128,4096]{2,1,0:T(8,128)(2,1)} copy(bf16[2,128,4096]{1,2,0:T(8,128)(2,1)S(1)} %pad_maximum_fusion) | data formatting | bytes 4194304
  231.8 11.7 %all-to-all-done.1 = f32[8,32,1024]{2,1,0:T(8,128)S(1)} async-done(((f32[8,32,1024]{2,1,0:T(8,128)}), f32[8,32,1024]{2,1,0:T(8,128)S(1)}, u32[]{:S(2)}, u32[]{:S(2)}) %all-to-all-start.1) | async-done | bytes 1048608 | tf_op jit(solution)/shard_map/all_to_all | solution.py:32
  (113 shorter events, 22.2 us)
Async XLA Ops:
  7.2 90.3 %all-gather.2.cloned.1.call-start = ((), (), s32[]{:S(2)}) async-start(), calls=%async_computation.2 | async-start | bytes 2162688 | tf_op jit(solution)/shard_map/all_gather | solution.py:91
  8.2 38.2 %collective-permute-start = (bf16[128,1024]{1,0:T(8,128)(2,1)S(1)}, bf16[128,1024]{1,0:T(8,128)(2,1)}, u32[]{:S(2)}, u32[]{:S(2)}) collective-permute-start(bf16[128,1024]{1,0:T(8,128)(2,1)S(1)} %slice_bitcast_fusion), channel_id=1, source_target_pairs={{16,0},{17,1},{18,2},{19,3},{20,4},{21,5},{22,6},{23,7},{24,8},{25... | collective-permute-start | bytes 786440 | tf_op jit(solution)/shard_map/ppermute | solution.py:15
  11.9 6.5 %copy-start.39 = (s32[2]{0:T(128)S(1)}, s32[2]{0:T(128)}, u32[]{:S(2)}) copy-start(s32[2]{0:T(128)} %param.10) | copy-start | bytes 28
  11.9 16.3 %collective-permute-start.1 = (s32[1]{0:T(128)}, s32[1]{0:T(128)}, u32[]{:S(2)}, u32[]{:S(2)}) collective-permute-start(s32[1]{0:T(128)} %get-tuple-element.28), channel_id=1, source_target_pairs={{16,0},{17,1},{18,2},{19,3},{20,4},{21,5},{22,6},{23,7},{24,8},{25... | collective-permute-start | bytes 20 | tf_op jit(solution)/shard_map/ppermute | solution.py:15
  16.2 31.3 %collective-permute-start.2 = (bf16[128,4096]{0,1:T(8,128)(2,1)}, bf16[128,4096]{0,1:T(8,128)(2,1)}, u32[]{:S(2)}, u32[]{:S(2)}) collective-permute-start(bf16[128,4096]{0,1:T(8,128)(2,1)} %bitcast.7), channel_id=1, source_target_pairs={{16,0},{17,1},{18,2},{19,3},{20,4},{21,5},{22,6},{23,7},{24,8},{25... | collective-permute-start | bytes 3145736 | tf_op jit(solution)/shard_map/ppermute | solution.py:15
  19.0 26.0 %collective-permute-start.3 = (s32[1]{0:T(128)}, s32[1]{0:T(128)}, u32[]{:S(2)}, u32[]{:S(2)}) collective-permute-start(s32[1]{0:T(128)} %get-tuple-element.30), channel_id=1, source_target_pairs={{16,0},{17,1},{18,2},{19,3},{20,4},{21,5},{22,6},{23,7},{24,8},{25... | collective-permute-start | bytes 20 | tf_op jit(solution)/shard_map/ppermute | solution.py:15
  23.3 42.6 %collective-permute-start.4 = (bf16[128,4096]{0,1:T(8,128)(2,1)}, bf16[128,4096]{0,1:T(8,128)(2,1)}, u32[]{:S(2)}, u32[]{:S(2)}) collective-permute-start(bf16[128,4096]{0,1:T(8,128)(2,1)} %bitcast.293), channel_id=1, source_target_pairs={{16,0},{17,1},{18,2},{19,3},{20,4},{21,5},{22,6},{23,7},{24,8},{25... | collective-permute-start | bytes 3145736 | tf_op jit(solution)/shard_map/ppermute | solution.py:15
  48.5 51.3 %copy-start.33 = (bf16[128,1024]{0,1:T(8,128)(2,1)}, bf16[128,1024]{0,1:T(8,128)(2,1)S(1)}, u32[]{:S(2)}) copy-start(bf16[128,1024]{0,1:T(8,128)(2,1)S(1)} %get-tuple-element.20) | copy-start | bytes 786436
  99.8 4.4 %copy-start.25 = (bf16[1152,128]{1,0:T(8,128)(2,1)}, bf16[1152,128]{1,0:T(8,128)(2,1)S(1)}, u32[]{:S(2)}) copy-start(bf16[1152,128]{1,0:T(8,128)(2,1)S(1)} %get-tuple-element.11) | copy-start | bytes 884740
  104.2 3.1 %copy-start.4 = (bf16[1024,1024]{1,0:T(8,128)(2,1)S(1)}, bf16[1024,1024]{1,0:T(8,128)(2,1)}, u32[]{:S(2)}) copy-start(bf16[1024,1024]{1,0:T(8,128)(2,1)} %all-gather.2.cloned.1.call-done) | copy-start | bytes 6291460
  107.3 2.3 copy-start.20
  107.4 2.3 copy-start.37
  109.7 1.3 copy-start.34
  111.0 1.6 copy-start.7
  118.0 3.1 %copy-start.5 = (bf16[1024,1024]{1,0:T(8,128)(2,1)S(1)}, bf16[1024,1024]{1,0:T(8,128)(2,1)}, u32[]{:S(2)}) copy-start(bf16[1024,1024]{1,0:T(8,128)(2,1)} %all-gather.2.cloned.1.call-done) | copy-start | bytes 6291460
  121.2 1.5 copy-start
  121.2 3.2 %copy-start.21 = (f32[8,128,1152]{1,2,0:T(8,128)S(1)}, f32[8,128,1152]{1,2,0:T(8,128)}, u32[]{:S(2)}) copy-start(f32[8,128,1152]{1,2,0:T(8,128)} %get-tuple-element.37) | copy-start | bytes 14155780
  121.2 3.2 %copy-start.38 = (f32[8,128]{1,0:T(8,128)S(1)}, f32[8,128]{1,0:T(8,128)}, u32[]{:S(2)}) copy-start(f32[8,128]{1,0:T(8,128)} %get-tuple-element.36) | copy-start | bytes 12292
  124.4 1.3 copy-start.32
  125.7 1.5 copy-start.9
  132.7 3.4 %copy-start.6 = (bf16[1024,1024]{1,0:T(8,128)(2,1)S(1)}, bf16[1024,1024]{1,0:T(8,128)(2,1)}, u32[]{:S(2)}) copy-start(bf16[1024,1024]{1,0:T(8,128)(2,1)} %all-gather.2.cloned.1.call-done) | copy-start | bytes 6291460
  136.0 1.4 copy-start.2
  136.0 3.2 %copy-start.19 = (f32[8,128,1152]{1,2,0:T(8,128)S(1)}, f32[8,128,1152]{1,2,0:T(8,128)}, u32[]{:S(2)}) copy-start(f32[8,128,1152]{1,2,0:T(8,128)} %get-tuple-element.35) | copy-start | bytes 14155780
  136.0 3.2 %copy-start.36 = (f32[8,128]{1,0:T(8,128)S(1)}, f32[8,128]{1,0:T(8,128)}, u32[]{:S(2)}) copy-start(f32[8,128]{1,0:T(8,128)} %get-tuple-element.34) | copy-start | bytes 12292
  139.2 1.3 copy-start.31
  140.6 1.6 copy-start.11
  140.6 1.6 copy-start.29
  147.5 3.2 %copy-start.26 = (bf16[1152,128,1]{1,0,2:T(8,128)(2,1)S(1)}, bf16[1152,128,1]{1,0,2:T(8,128)(2,1)}, u32[]{:S(2)}) copy-start(bf16[1152,128,1]{1,0,2:T(8,128)(2,1)} %get-tuple-element.14) | copy-start | bytes 884740
  147.5 4.7 %copy-start.18 = (f32[8,128,1152]{1,2,0:T(8,128)S(1)}, f32[8,128,1152]{1,2,0:T(8,128)}, u32[]{:S(2)}) copy-start(f32[8,128,1152]{1,2,0:T(8,128)} %get-tuple-element.33) | copy-start | bytes 14155780
  150.6 1.6 copy-start.28
  150.6 1.6 copy-start.35
  152.2 1.7 copy-start.16
  152.2 1.7 copy-start.30
  153.9 1.4 copy-start.13
  155.4 1.7 copy-start.1
  157.0 1.7 copy-start.3
  160.5 2.1 copy-start.17
  162.6 12.0 %copy-start.8 = (bf16[8,128,1152]{1,2,0:T(8,128)(2,1)S(1)}, bf16[8,128,1152]{1,2,0:T(8,128)(2,1)}, u32[]{:S(2)}) copy-start(bf16[8,128,1152]{1,2,0:T(8,128)(2,1)} %copy-done.7) | copy-start | bytes 7077892
  162.6 57.0 %all-to-all-start = ((bf16[32,32,1024]{2,1,0:T(8,128)(2,1)}), bf16[32,32,1024]{2,1,0:T(8,128)(2,1)}, u32[]{:S(2)}, u32[]{:S(2)}) async-start(bf16[32,32,1024]{2,1,0:T(8,128)(2,1)} %bitcast.275), calls=%async_computation | async-start | bytes 4194304 | tf_op jit(solution)/shard_map/all_to_all | solution.py:26
  169.9 6.2 %copy-start.24 = (bf16[1152,128]{1,0:T(8,128)(2,1)S(1)}, bf16[1152,128]{1,0:T(8,128)(2,1)}, u32[]{:S(2)}) copy-start(bf16[1152,128]{1,0:T(8,128)(2,1)} %get-tuple-element.12) | copy-start | bytes 884740
  170.6 5.6 %copy-start.10 = (bf16[8,128,1152]{1,2,0:T(8,128)(2,1)S(1)}, bf16[8,128,1152]{1,2,0:T(8,128)(2,1)}, u32[]{:S(2)}) copy-start(bf16[8,128,1152]{1,2,0:T(8,128)(2,1)} %copy-done.9) | copy-start | bytes 7077892
  172.5 4.2 %copy-start.12 = (bf16[8,128,1152]{1,2,0:T(8,128)(2,1)S(1)}, bf16[8,128,1152]{1,2,0:T(8,128)(2,1)}, u32[]{:S(2)}) copy-start(bf16[8,128,1152]{1,2,0:T(8,128)(2,1)} %copy-done.11) | copy-start | bytes 7077892
  172.5 4.2 %copy-start.23 = (bf16[1152,128]{1,0:T(8,128)(2,1)S(1)}, bf16[1152,128]{1,0:T(8,128)(2,1)}, u32[]{:S(2)}) copy-start(bf16[1152,128]{1,0:T(8,128)(2,1)} %get-tuple-element.13) | copy-start | bytes 884740
  172.5 54.7 %collective-permute-start.6 = (bf16[128,1024]{1,0:T(8,128)(2,1)}, bf16[128,1024]{1,0:T(8,128)(2,1)}, u32[]{:S(2)}, u32[]{:S(2)}) collective-permute-start(bf16[128,1024]{1,0:T(8,128)(2,1)} %get-tuple-element.10), channel_id=1, source_target_pairs={{16,0},{17,1},{18,2},{19,3},{20,4},{21,5},{22,6},{23,7},{24,8},{25... | collective-permute-start | bytes 786440 | tf_op jit(solution)/shard_map/ppermute | solution.py:15
  176.2 1.7 copy-start.14
  176.2 1.7 copy-start.22
  179.5 49.3 %collective-permute-start.5 = (bf16[128,4096]{0,1:T(8,128)(2,1)}, bf16[128,4096]{0,1:T(8,128)(2,1)S(1)}, u32[]{:S(2)}, u32[]{:S(2)}) collective-permute-start(bf16[128,4096]{0,1:T(8,128)(2,1)} %pad_maximum_fusion.1), channel_id=1, source_target_pairs={{16,0},{17,1},{18,2},{19,3},{20,4},{21,5},{22,6},{23,7},{24,8},{25... | collective-permute-start | bytes 3145736 | tf_op jit(solution)/shard_map/ppermute | solution.py:15
  222.7 20.8 %all-to-all-start.1 = ((f32[8,32,1024]{2,1,0:T(8,128)}), f32[8,32,1024]{2,1,0:T(8,128)S(1)}, u32[]{:S(2)}, u32[]{:S(2)}) async-start(f32[8,32,1024]{2,1,0:T(8,128)} %broadcast_in_dim.54), calls=%async_computation.1 | async-start | bytes 2097152 | tf_op jit(solution)/shard_map/all_to_all | solution.py:32
  (2 other events, 1.9 us)
Sparse Core Ops, SparseCore 0:
  10.7 86.7 all-gather.1
where the time goes:
time: 252 us; the launch traced here: 251 us
  waiting for transfers between devices  112 us (44%)
  matrix products  41.3 us (16%)
  local copies, waits for them, and re-layouts  29.5 us (12%)
  other arithmetic  25.2 us (10%)
  starting transfers between devices  24.5 us (10%)
  between operations  18.5 us (7%)
    all_to_all x1, waiting for transfers between devices, summed_on_arrival(): lax.all_to_all(blocks, axis, split_axis=0, concat_axis=0, tiled=True)  38.8 us
    ppermute x7, waiting for transfers between devices, passed_along(): return lax.ppermute(block, axis, route)  31.7 us
    all_gather x1, waiting for transfers between devices, local(): root_keys = lax.all_gather(root_kv, 'dev', axis=0, tiled=True)  29.8 us
    sub x4, matrix products, tile_grads(): weights = jnp.exp(scores - peak)  20.5 us
    unnamed x85, local copies, waits for them, and re-layouts  18.8 us
    ppermute x7, starting transfers between devices, passed_along(): return lax.ppermute(block, axis, route)  13 us
    convert_element_type x4, other arithmetic, tile_grads(): probs = weights.astype(jnp.bfloat16)  12.7 us
    all_to_all x1, waiting for transfers between devices, from_everyone(): return lax.all_to_all(copies, axis, split_axis=0, concat_axis=0, tiled=True)  11.7 us
  transfers between devices with their start and end apart: 10, of which 5 were waited for; matrix products, arithmetic and copies ran while one was open for 11% of the time, Pallas kernels for 0%

commit v1 on v0

v1 whole, which is shorter than its diff:
```python
import functools
import math

import jax
import jax.numpy as jnp
from jax import lax
from jax.experimental import pallas as pl
from jax.experimental.pallas import tpu as pltpu
from jax.sharding import PartitionSpec as P

KVH = 4
GROUP = 8
DH = 128
TILE = 128
R = 1024
SEGS = 4
NX, NY, NZ = 4, 4, 8
CHUNKS = 2 * KVH
WIDTH = KVH * DH
SCALE = DH**-0.5
SCALE_LOG2 = SCALE * math.log2(math.e)
PACK = 4

F32 = jnp.float32
BF16 = jnp.bfloat16
MESH = pl.DeviceIdType.MESH
NT = (((1,), (1,)), ((), ()))
NN = (((1,), (0,)), ((), ()))


def dot(a, b, dims):
    return lax.dot_general(a, b, dims, preferred_element_type=F32)


def softmax_grads(q, g, segment, keys, values, branch_keys, branch_values, p_ref, ds_ref):
    rows = PACK * TILE
    row_pos = lax.rem(lax.broadcasted_iota(jnp.int32, (rows, TILE), 0), TILE)
    col_pos = lax.broadcasted_iota(jnp.int32, (rows, TILE), 1)
    part = R // SEGS
    s_root = [dot(q, keys[b * part : (b + 1) * part], NT) for b in range(SEGS)]
    s_branch = jnp.where(col_pos <= row_pos, dot(q, branch_keys, NT), F32(-1e30))
    peak = jnp.maximum(
        jnp.max(s_branch, axis=1, keepdims=True), jnp.max(s_root[0], axis=1, keepdims=True)
    )
    for b in range(1, SEGS):
        of_part = jnp.max(s_root[b], axis=1, keepdims=True)
        peak = jnp.maximum(peak, jnp.where(b <= segment, of_part, F32(-1e30)))
    shift = peak * SCALE_LOG2
    w_branch = jnp.exp2(s_branch * SCALE_LOG2 - shift)
    total = jnp.sum(w_branch, axis=1, keepdims=True)
    w_root = []
    for b in range(SEGS):
        own_shift = shift if b == 0 else jnp.where(b <= segment, shift, F32(1e30))
        w = jnp.exp2(s_root[b] * SCALE_LOG2 - own_shift)
        total = total + jnp.sum(w, axis=1, keepdims=True)
        w_root.append(w)
    inverse = 1.0 / total
    w_branch = w_branch * inverse
    w_root = [w * inverse for w in w_root]
    d_branch = dot(g, branch_values, NT)
    d_root = [dot(g, values[b * part : (b + 1) * part], NT) for b in range(SEGS)]
    delta = jnp.sum(w_branch * d_branch, axis=1, keepdims=True)
    for b in range(SEGS):
        delta = delta + jnp.sum(w_root[b] * d_root[b], axis=1, keepdims=True)
    for b in range(SEGS):
        p_ref[:, b * part : (b + 1) * part] = w_root[b].astype(BF16)
        ds_ref[:, b * part : (b + 1) * part] = (w_root[b] * (d_root[b] - delta)).astype(BF16)
    p_ref[:, R:] = w_branch.astype(BF16)
    ds_ref[:, R:] = (w_branch * (d_branch - delta)).astype(BF16)


def kernel(
    lengths,
    segments,
    q_hbm,
    g_hbm,
    branch_hbm,
    root_ref,
    dq_hbm,
    db_hbm,
    out_ref,
    q_s,
    g_s,
    branch_s,
    kv,
    dq_s,
    db_s,
    p_s,
    ds_s,
    dk_acc,
    dv_acc,
    dpart,
    r0,
    s1,
    r1,
    s2,
    r2,
    in_sem,
    out_sem,
    z_send,
    z_recv,
    y_send,
    y_recv,
    c_send,
    c_recv,
    s0_send,
    s0_recv,
    s1_send,
    s1_recv,
    s2_send,
    s2_recv,
):
    grp = lax.axis_index("grp")
    dev = lax.axis_index("dev")
    x, z_lo = grp // 2, grp % 2
    y, z_hi, c = dev // 8, (dev // 2) % 4, dev % 2
    z = 2 * z_hi + z_lo

    def at(px, py, pz, pc):
        return (px * 2 + pz % 2, py * 8 + (pz // 2) * 2 + pc)

    def ring_z(offset):
        return (z + offset + NZ) % NZ

    away = 2 * z_lo - 1
    z_dests = [at(x, y, ring_z(away * k), c) for k in (1, 2, 3)]
    z_sources = [at(x, y, ring_z(away * k), c) for k in (1, 3, -2)]
    y_dests = [at(x, (y + k) % NY, z, c) for k in (1, 2, 3)]
    other_core = at(x, y, z, 1 - c)
    plane = [((x + k // NY) % NX, (y + k % NY) % NY) for k in range(1, NX * NY)]
    final_dests = [((x + k // 2) % NX, 2 * x + k % 2) for k in range(2 * NX)]

    q_copies = [pltpu.make_async_copy(q_hbm.at[t], q_s.at[t], in_sem.at[t]) for t in range(2)]
    g_copies = [pltpu.make_async_copy(g_hbm.at[t], g_s.at[t], in_sem.at[2 + t]) for t in range(2)]
    b_copy = pltpu.make_async_copy(branch_hbm, branch_s, in_sem.at[4])
    for copy in (b_copy, q_copies[0], g_copies[0], q_copies[1], g_copies[1]):
        copy.start()

    barrier = pltpu.get_barrier_semaphore()

    def greet(device):
        pl.semaphore_signal(barrier, inc=1, device_id=device, device_id_type=MESH)

    greet(other_core)
    for px, py in plane:
        greet(at(px, py, z, c))
    for device in z_dests + z_sources:
        greet(device)
    for px, pz in final_dests:
        own = jnp.logical_and(px == x, pz == z)
        pl.when(jnp.logical_not(own))(functools.partial(greet, at(px, y, pz, c)))
    for k in range(NZ):
        pz = (z + k) % NZ
        own = jnp.logical_and(z_hi == x, pz == z)
        pl.when(jnp.logical_not(own))(functools.partial(greet, at(z_hi, y, pz, c)))
    own_final = jnp.where(z_hi == x, 2, 0)
    pl.semaphore_wait(barrier, 1 + 15 + 6 + 16 - own_final)

    def remote(src, dst, send_sem, recv_sem, device):
        return pltpu.make_async_remote_copy(
            src_ref=src,
            dst_ref=dst,
            send_sem=send_sem,
            recv_sem=recv_sem,
            device_id=device,
            device_id_type=MESH,
        )

    def arrived(ref, sem):
        pltpu.make_async_copy(ref, ref, sem).wait()

    def gather_z(chunk):
        start = (chunk % 2) * WIDTH + (chunk // 2) * DH
        src = root_ref.at[:, start : start + DH]
        dst = kv.at[chunk, y, c, z_hi]
        pltpu.make_async_copy(src, dst, z_recv.at[chunk]).start()
        for device in z_dests:
            remote(src, dst, z_send, z_recv.at[chunk], device).start()

    def gather_y(chunk):
        block = kv.at[chunk, y, c]
        arrived(block, z_recv.at[chunk])
        for device in y_dests:
            remote(block, block, y_send, y_recv.at[chunk], device).start()

    def gather_core(chunk):
        arrived(kv.at[chunk, pl.ds(0, 3), c], y_recv.at[chunk])
        block = kv.at[chunk, :, c]
        remote(block, block, c_send, c_recv.at[chunk], other_core).start()

    def gathered(chunk):
        arrived(kv.at[chunk, :, 1 - c], c_recv.at[chunk])

    def reduce_core(chunk):
        remote(dpart.at[chunk, :, 1 - c], r0.at[chunk], s0_send, s0_recv.at[chunk], other_core).start()

    def reduce_plane(chunk):
        arrived(r0.at[chunk], s0_recv.at[chunk])
        s1[chunk] = (dpart[chunk, :, c].astype(F32) + r0[chunk].astype(F32)).astype(BF16)
        for k, (px, py) in enumerate(plane):
            remote(
                s1.at[chunk, py, px], r1.at[chunk, k], s1_send, s1_recv.at[chunk], at(px, py, z, c)
            ).start()

    def reduce_groups(chunk):
        arrived(r1.at[chunk], s1_recv.at[chunk])
        s2[chunk] = (s1[chunk, y, x].astype(F32) + jnp.sum(r1[chunk].astype(F32), axis=0)).astype(BF16)
        for px, pz in final_dests:
            own = jnp.logical_and(px == x, pz == z)

            @pl.when(own)
            def _():
                pltpu.make_async_copy(s2.at[chunk], r2.at[chunk, z], s2_recv.at[chunk]).start()

            @pl.when(jnp.logical_not(own))
            def _():
                remote(s2.at[chunk], r2.at[chunk, z], s2_send, s2_recv.at[chunk], at(px, y, pz, c)).start()

    def reduce_done(chunk):
        arrived(r2.at[chunk], s2_recv.at[chunk])
        start = pl.multiple_of((chunk % 2) * WIDTH + (chunk // 2) * DH, DH)
        out_ref[:, pl.ds(start, DH)] = jnp.sum(r2[chunk].astype(F32), axis=0)

    for chunk in range(CHUNKS):
        gather_z(chunk)
    gather_y(0)
    gather_y(1)
    gather_core(0)
    gather_core(1)
    b_copy.wait()
    gathered(0)
    gathered(1)

    def both(stage, head):
        stage(2 * head + 1)
        stage(2 * head)

    def step(index, carry):
        head, t = index // 2, index % 2

        @pl.when(index == 0)
        def _():
            q_copies[0].wait()
            g_copies[0].wait()

        @pl.when(index == 1)
        def _():
            q_copies[1].wait()
            g_copies[1].wait()

        @pl.when(jnp.logical_and(t == 0, head > 0))
        def _():
            gathered(2 * head)
            gathered(2 * head + 1)

        @pl.when(jnp.logical_and(t == 0, head < KVH - 1))
        def _():
            gather_y(2 * head + 2)
            gather_y(2 * head + 3)

        @pl.when(jnp.logical_and(t == 1, head < KVH - 1))
        def _():
            gather_core(2 * head + 2)
            gather_core(2 * head + 3)

        length, segment = lengths[t], segments[t]
        live = lax.broadcasted_iota(jnp.int32, (TILE, DH), 0) < length
        keys = kv[2 * head].reshape(R, DH)
        values = kv[2 * head + 1].reshape(R, DH)
        k_cols = pl.ds(pl.multiple_of(head * DH, DH), DH)
        v_cols = pl.ds(pl.multiple_of(WIDTH + head * DH, DH), DH)
        branch_keys = branch_s[t, :, k_cols]
        branch_values = branch_s[t, :, v_cols]
        q_t, g_t = [], []
        for first in range(0, GROUP, PACK):
            qs, gs = [], []
            for j in range(first, first + PACK):
                cols = pl.ds(pl.multiple_of((head * GROUP + j) * DH, DH), DH)
                qs.append(q_s[t, :, cols])
                gs.append(jnp.where(live, g_s[t, :, cols], jnp.zeros((), BF16)))
            rows = pl.ds(first * TILE, PACK * TILE)
            softmax_grads(
                jnp.concatenate(qs, axis=0),
                jnp.concatenate(gs, axis=0),
                segment,
                keys,
                values,
                branch_keys,
                branch_values,
                p_s.at[rows],
                ds_s.at[rows],
            )
            dq = dot(ds_s[rows, :R], keys, NN) + dot(ds_s[rows, R:], branch_keys, NN)
            dq = (dq * SCALE).astype(BF16)
            for j in range(PACK):
                cols = pl.ds(pl.multiple_of((head * GROUP + first + j) * DH, DH), DH)
                dq_s[t, :, cols] = dq[j * TILE : (j + 1) * TILE]
            q_t += [block.T for block in qs]
            g_t += [block.T for block in gs]
        dk = dot(jnp.concatenate(q_t, axis=1), ds_s[...], NN) * SCALE
        dv = dot(jnp.concatenate(g_t, axis=1), p_s[...], NN)
        db_s[t, :, k_cols] = dk[:, R:].T.astype(BF16)
        db_s[t, :, v_cols] = dv[:, R:].T.astype(BF16)
        heads = pl.ds(pl.multiple_of(head * GROUP * DH, GROUP * DH), GROUP * DH)
        pltpu.make_async_copy(dq_s.at[t, :, heads], dq_hbm.at[t, :, heads], out_sem.at[0]).start()

        @pl.when(t == 0)
        def _():
            dk_acc[...] = dk[:, :R]
            dv_acc[...] = dv[:, :R]

        @pl.when(t == 1)
        def _():
            shape = (NY, 2, NZ // 2, R // 32, DH)
            dpart[2 * head + 1] = (dv_acc[...] + dv[:, :R]).T.astype(BF16).reshape(shape)
            reduce_core(2 * head + 1)
            dpart[2 * head] = (dk_acc[...] + dk[:, :R]).T.astype(BF16).reshape(shape)
            reduce_core(2 * head)

        @pl.when(jnp.logical_and(t == 0, head >= 2))
        def _():
            both(reduce_done, head - 2)

        @pl.when(jnp.logical_and(t == 0, head >= 1))
        def _():
            both(reduce_plane, head - 1)

        @pl.when(jnp.logical_and(t == 1, head >= 1))
        def _():
            both(reduce_groups, head - 1)

        return carry

    lax.fori_loop(0, 2 * KVH, step, 0)
    db_copy = pltpu.make_async_copy(db_s, db_hbm, out_sem.at[1])
    db_copy.start()
    both(reduce_plane, KVH - 1)
    both(reduce_done, KVH - 2)
    both(reduce_groups, KVH - 1)
    both(reduce_done, KVH - 1)

    arrived(dq_s, out_sem.at[0])
    db_copy.wait()
    for _ in range(3):
        arrived(kv.at[:, 0, 0, 0], z_send)
        arrived(kv.at[:, 0, 0], y_send)
    arrived(kv.at[:, :, 0], c_send)
    arrived(r0, s0_send)
    arrived(r1, s1_send)

    @pl.when(z_hi == x)
    def _():
        arrived(r2.at[:, pl.ds(0, 7)], s2_send)

    @pl.when(z_hi != x)
    def _():
        arrived(r2, s2_send)


def local(query, grad_out, branch_kv, root_kv, lengths, segments):
    rows = R // 32
    anywhere = pl.BlockSpec(memory_space=pl.ANY)
    vmem = pl.BlockSpec(memory_space=pltpu.VMEM)
    smem = pl.BlockSpec(memory_space=pltpu.SMEM)
    dma = pltpu.SemaphoreType.DMA
    blocks = (CHUNKS, NY, 2, NZ // 2, rows, DH)
    half = (CHUNKS, NY, NZ // 2, rows, DH)
    return pl.pallas_call(
        kernel,
        out_shape=(
            jax.ShapeDtypeStruct(query.shape, BF16),
            jax.ShapeDtypeStruct(branch_kv.shape, BF16),
            jax.ShapeDtypeStruct(root_kv.shape, F32),
        ),
        in_specs=[smem, smem, anywhere, anywhere, anywhere, vmem],
        out_specs=(anywhere, anywhere, vmem),
        scratch_shapes=[
            pltpu.VMEM(query.shape, BF16),
            pltpu.VMEM(query.shape, BF16),
            pltpu.VMEM(branch_kv.shape, BF16),
            pltpu.VMEM(blocks, BF16),
            pltpu.VMEM(query.shape, BF16),
            pltpu.VMEM(branch_kv.shape, BF16),
            pltpu.VMEM((GROUP * TILE, R + TILE), BF16),
            pltpu.VMEM((GROUP * TILE, R + TILE), BF16),
            pltpu.VMEM((DH, R), F32),
            pltpu.VMEM((DH, R), F32),
            pltpu.VMEM(blocks, BF16),
            pltpu.VMEM(half, BF16),
            pltpu.VMEM(half, BF16),
            pltpu.VMEM((CHUNKS, NX * NY - 1, rows, DH), BF16),
            pltpu.VMEM((CHUNKS, rows, DH), BF16),
            pltpu.VMEM((CHUNKS, NZ, rows, DH), BF16),
            dma((5,)),
            dma((2,)),
            dma,
            dma((CHUNKS,)),
            dma,
            dma((CHUNKS,)),
            dma,
            dma((CHUNKS,)),
            dma,
            dma((CHUNKS,)),
            dma,
            dma((CHUNKS,)),
            dma,
            dma((CHUNKS,)),
        ],
        compiler_params=pltpu.CompilerParams(
            collective_id=0, has_side_effects=True, vmem_limit_bytes=60 << 20
        ),
    )(lengths, segments, query, grad_out, branch_kv, root_kv)


def solution(mesh):
    placed = (
        P(("grp", "dev"), None, None),
        P(("grp", "dev"), None, None),
        P(("grp", "dev"), None, None),
        P("dev", None),
        P(("grp", "dev")),
        P(("grp", "dev")),
    )
    return jax.shard_map(
        local,
        mesh=mesh,
        in_specs=placed,
        out_specs=(P(("grp", "dev"), None, None), P(("grp", "dev"), None, None), P("dev", None)),
        check_vma=False,
    )
```

time: 252 us -> 104 us (0.41)
  waiting for transfers between devices: 112 us -> 0 us
  Pallas kernels: 0 us -> 97.4 us
  matrix products: 41.3 us -> 0 us
  other arithmetic: 25.2 us -> 0 us
  local copies, waits for them, and re-layouts: 29.5 us -> 4.65 us
  starting transfers between devices: 24.5 us -> 0 us
  between operations: 18.5 us -> 0.66 us
    pallas_call x0 -> x1, Pallas kernels: none -> 97.4 us  [local(): pl.pallas_call(kernel, out_shape=(jax.ShapeDtypeStruct(query.shape, BF16)...]
    all_to_all x2 -> x0, waiting for transfers between devices: 50.5 us -> none  [the longest x1 38.8 us: summed_on_arrival(): lax.all_to_all(blocks, axis, split_axis=0, concat_axis=0, tiled=True)]
    ppermute x7 -> x0, waiting for transfers between devices: 31.7 us -> none  [passed_along(): return lax.ppermute(block, axis, route)]
    all_gather x1 -> x0, waiting for transfers between devices: 29.8 us -> none  [local(): root_keys = lax.all_gather(root_kv, 'dev', axis=0, tiled=True)]
    dot_general x20 -> x0, matrix products: 20.8 us -> none  [the longest x4 5.57 us: tile_grads(): jnp.einsum('gtl,tgd->ld', score_grad, q_head, preferred_element_type=jnp....]
    sub x4 -> x0, matrix products: 20.5 us -> none  [tile_grads(): weights = jnp.exp(scores - peak)]
    unnamed x85 -> x7, local copies, waits for them, and re-layouts: 18.8 us -> 4.65 us
    ppermute x7 -> x0, starting transfers between devices: 13 us -> none  [passed_along(): return lax.ppermute(block, axis, route)]
  transfers between devices with their start and end apart: 10 -> 0, of which waited for: 5 -> 0; matrix products, arithmetic and copies ran while one was open for 11% -> 0% of each run, Pallas kernels for 0% -> 0%
where the time goes in v1:
time: 104 us; the launch traced here: 103 us
  Pallas kernels  97.4 us (94%)
  local copies, waits for them, and re-layouts  4.65 us (4%)
    pallas_call x1, Pallas kernels, local(): pl.pallas_call(kernel, out_shape=(jax.ShapeDtypeStruct(query.shape, BF16)...  97.4 us
    unnamed x7, local copies, waits for them, and re-layouts  4.65 us

profile of v1, /device:TPU:8, one launch (start us, length us, event | category | flops | bytes accessed | tf_op | source)
XLA Modules:
  0.0 102.7 jit_solution(9221976521762602606)
XLA Ops:
  0.6 97.4 %shard_map.85 = (bf16[2,128,4096]{2,1,0:T(8,128)(2,1)}, bf16[2,128,1024]{2,1,0:T(8,128)(2,1)}, f32[32,1024]{1,0:T(8,128)}) custom-call(s32[2]{0:T(128)} %lengths.1, s32[2]{0:T(128)} %segments.1, bf16[2,128,4096]{2,1,0:T(8,128)(2,1)} %q_hbm.1, bf16[2,128,4096]{2,1,0:T(8,128)(2,1)} %g_hbm.1, bf16[2,128,1024]{2,1,0:T(8,128)(2,1)} %branch_hbm.1, ...), custom_call_target="tpu_custom_call" | custom-call | tf_op jit(solution)/shard_map/pallas_call | solution.py:368
  98.0 0.0 copy-start
  98.0 0.0 copy-start.1
  98.1 3.2 %copy.12 = bf16[2,128,4096]{2,1,0:T(8,128)(2,1)} copy(bf16[2,128,4096]{2,1,0:T(8,128)(2,1)} %get-tuple-element.6) | data formatting | bytes 4194304
  101.3 0.0 copy-done
  101.3 0.8 copy.13
  102.0 0.0 copy-done.1
  102.1 0.7 copy.14
Async XLA Ops:
  98.0 3.2 %copy-start = (bf16[2,128,1024]{2,1,0:T(8,128)(2,1)S(1)}, bf16[2,128,1024]{2,1,0:T(8,128)(2,1)}, u32[]{:S(2)}) copy-start(bf16[2,128,1024]{2,1,0:T(8,128)(2,1)} %get-tuple-element.7) | copy-start | bytes 1572868
  98.0 4.0 %copy-start.1 = (f32[32,1024]{1,0:T(8,128)S(1)}, f32[32,1024]{1,0:T(8,128)}, u32[]{:S(2)}) copy-start(f32[32,1024]{1,0:T(8,128)} %get-tuple-element.8) | copy-start | bytes 393220

commit v2 on v1

v2 whole, which is shorter than its diff:
```python
import functools
import math

import jax
import jax.numpy as jnp
from jax import lax
from jax.experimental import pallas as pl
from jax.experimental.pallas import tpu as pltpu
from jax.sharding import PartitionSpec as P

KVH = 4
GROUP = 8
DH = 128
TILE = 128
R = 1024
SEGS = 4
NX, NY, NZ = 4, 4, 8
CHUNKS = 2 * KVH
WIDTH = KVH * DH
SCALE = DH**-0.5
SCALE_LOG2 = SCALE * math.log2(math.e)
PACK = 4
ROWS = 16
AHEAD = 3

F32 = jnp.float32
BF16 = jnp.bfloat16
MESH = pl.DeviceIdType.MESH
NT = (((1,), (1,)), ((), ()))
NN = (((1,), (0,)), ((), ()))


def dot(a, b, dims):
    return lax.dot_general(a, b, dims, preferred_element_type=F32)


TILES = R // DH + 1
OF_PART = R // SEGS // DH


def tile_of(ref, first, b):
    return ref[pl.ds(first, ROWS), b * DH : (b + 1) * DH]


def across(x, reduce):
    return jnp.broadcast_to(reduce(x, axis=1, keepdims=True), (ROWS, DH))


def peaks(first, segment, s_ref, stats):
    row_pos = first % TILE + lax.broadcasted_iota(jnp.int32, (ROWS, DH), 0)
    col_pos = lax.broadcasted_iota(jnp.int32, (ROWS, DH), 1)
    branch = jnp.where(col_pos <= row_pos, tile_of(s_ref, first, TILES - 1), F32(-1e30))
    peak = branch
    for part in range(SEGS):
        top = tile_of(s_ref, first, part * OF_PART)
        for b in range(part * OF_PART + 1, (part + 1) * OF_PART):
            top = jnp.maximum(top, tile_of(s_ref, first, b))
        seen = top if part == 0 else jnp.where(part <= segment, top, F32(-1e30))
        peak = jnp.maximum(peak, seen)
    stats[0, pl.ds(first, ROWS)] = across(peak, jnp.max) * SCALE_LOG2


def exponentials(first, segment, s_ref, d_ref, stats):
    rows = pl.ds(first, ROWS)
    row_pos = first % TILE + lax.broadcasted_iota(jnp.int32, (ROWS, DH), 0)
    col_pos = lax.broadcasted_iota(jnp.int32, (ROWS, DH), 1)
    shift = stats[0, rows]
    total = delta = None
    for b in range(TILES):
        score = tile_of(s_ref, first, b)
        own_shift = shift
        if b == TILES - 1:
            own_shift = jnp.where(col_pos <= row_pos, shift, F32(1e30))
        elif b >= OF_PART:
            own_shift = jnp.where(b // OF_PART <= segment, shift, F32(1e30))
        e = jnp.exp2(score * SCALE_LOG2 - own_shift)
        s_ref[rows, b * DH : (b + 1) * DH] = e
        term = e * tile_of(d_ref, first, b)
        total = e if total is None else total + e
        delta = term if delta is None else delta + term
    inverse = 1.0 / across(total, jnp.sum)
    stats[1, rows] = inverse
    stats[2, rows] = across(delta, jnp.sum) * inverse


def weigh(first, s_ref, d_ref, p_ref, ds_ref, stats):
    rows = pl.ds(first, ROWS)
    inverse, delta = stats[1, rows], stats[2, rows]
    for b in range(TILES):
        cols = slice(b * DH, (b + 1) * DH)
        w = tile_of(s_ref, first, b) * inverse
        p_ref[rows, cols] = w.astype(BF16)
        ds_ref[rows, cols] = (w * (tile_of(d_ref, first, b) - delta)).astype(BF16)


def interleaved(many, few):
    done = 0
    for i, piece in enumerate(many):
        piece()
        while done < len(few) and (done + 1) * len(many) <= (i + 1) * len(few):
            few[done]()
            done += 1
    assert done == len(few)


def kernel(
    lengths,
    segments,
    q_hbm,
    g_hbm,
    branch_hbm,
    root_ref,
    dq_ref,
    db_ref,
    out_ref,
    q_s,
    g_s,
    branch_s,
    kv,
    sa,
    sb,
    da,
    db,
    pa,
    pb,
    ds_a,
    ds_b,
    q_t,
    g_t,
    acc,
    branch_acc,
    stats,
    dpart,
    r0,
    s1,
    r1,
    s2,
    r2,
    s3,
    r3,
    in_sem,
    z_send,
    z_recv,
    y_send,
    y_recv,
    c_send,
    c_recv,
    s0_send,
    s0_recv,
    s1_send,
    s1_recv,
    s2_send,
    s2_recv,
    s3_send,
    s3_recv,
):
    grp = lax.axis_index("grp")
    dev = lax.axis_index("dev")
    x, z_lo = grp // 2, grp % 2
    y, z_hi, c = dev // 8, (dev // 2) % 4, dev % 2
    z = 2 * z_hi + z_lo

    def at(px, py, pz, pc):
        return (px * 2 + pz % 2, py * 8 + (pz // 2) * 2 + pc)

    def ring_z(offset):
        return (z + offset + NZ) % NZ

    away = 2 * z_lo - 1
    z_dests = [at(x, y, ring_z(away * k), c) for k in (1, 2, 3)]
    y_dests = [at(x, (y + k) % NY, z, c) for k in (1, 2, 3)]
    other_core = at(x, y, z, 1 - c)
    plane = [((x + k // NY) % NX, (y + k % NY) % NY) for k in range(1, NX * NY)]
    column = [(z + k) % NZ for k in range(1, NZ)]
    x_dests = [at((x + k) % NX, y, z, c) for k in (1, 2, 3)]

    q_copies = [pltpu.make_async_copy(q_hbm.at[t], q_s.at[t], in_sem.at[t]) for t in range(2)]
    g_copies = [pltpu.make_async_copy(g_hbm.at[t], g_s.at[t], in_sem.at[2 + t]) for t in range(2)]
    b_copy = pltpu.make_async_copy(branch_hbm, branch_s, in_sem.at[4])
    for copy in (b_copy, q_copies[0], g_copies[0], q_copies[1], g_copies[1]):
        copy.start()

    barrier = pltpu.get_barrier_semaphore()

    def greet(device):
        pl.semaphore_signal(barrier, inc=1, device_id=device, device_id_type=MESH)

    greet(other_core)
    for px, py in plane:
        greet(at(px, py, z, c))
    for pz in column:
        greet(at(x, y, pz, c))
    pl.semaphore_wait(barrier, 1 + len(plane) + len(column))

    def remote(src, dst, send_sem, recv_sem, device):
        return pltpu.make_async_remote_copy(
            src_ref=src,
            dst_ref=dst,
            send_sem=send_sem,
            recv_sem=recv_sem,
            device_id=device,
            device_id_type=MESH,
        )

    def arrived(ref, sem):
        pltpu.make_async_copy(ref, ref, sem).wait()

    def gather_z(chunk):
        start = (chunk % 2) * WIDTH + (chunk // 2) * DH
        src = root_ref.at[:, start : start + DH]
        dst = kv.at[chunk, y, c, z_hi]
        pltpu.make_async_copy(src, dst, z_recv.at[chunk]).start()
        for device in z_dests:
            remote(src, dst, z_send, z_recv.at[chunk], device).start()

    def gather_y(chunk):
        block = kv.at[chunk, y, c]
        arrived(block, z_recv.at[chunk])
        for device in y_dests:
            remote(block, block, y_send, y_recv.at[chunk], device).start()

    def gather_core(chunk):
        arrived(kv.at[chunk, pl.ds(0, 3), c], y_recv.at[chunk])
        block = kv.at[chunk, :, c]
        remote(block, block, c_send, c_recv.at[chunk], other_core).start()

    def gathered(chunk):
        arrived(kv.at[chunk, :, 1 - c], c_recv.at[chunk])

    def reduce_core(head):
        remote(dpart.at[head, :, 1 - c], r0.at[head], s0_send, s0_recv.at[head], other_core).start()

    def reduce_plane(head):
        arrived(r0.at[head], s0_recv.at[head])
        s1[head] = (dpart[head, :, c].astype(F32) + r0[head].astype(F32)).astype(BF16)
        for k, (px, py) in enumerate(plane):
            remote(
                s1.at[head, py, px], r1.at[head, k], s1_send, s1_recv.at[head], at(px, py, z, c)
            ).start()

    def reduce_column(head):
        arrived(r1.at[head], s1_recv.at[head])
        s2[head] = (s1[head, y, x].astype(F32) + jnp.sum(r1[head].astype(F32), axis=0)).astype(BF16)
        for k, pz in enumerate(column):
            remote(
                s2.at[head, pz // 2], r2.at[head, k], s2_send, s2_recv.at[head], at(x, y, pz, c)
            ).start()

    def share_sum(head):
        arrived(r2.at[head], s2_recv.at[head])
        summed = s2[head, z_hi].astype(F32) + jnp.sum(r2[head].astype(F32), axis=0)
        s3[head] = summed
        r3[head, x] = summed
        for device in x_dests:
            remote(s3.at[head], r3.at[head, x], s3_send, s3_recv.at[head], device).start()

    def reduce_done(head):
        arrived(r3.at[head, pl.ds(0, 3)], s3_recv.at[head])
        for part in range(NX):
            cols = pl.ds(pl.multiple_of((part // 2) * WIDTH + head * DH, DH), DH)
            out_ref[(part % 2) * 16 : (part % 2 + 1) * 16, cols] = r3[head, part]

    ds_s = (ds_a, ds_b)

    def columns(first, count=1):
        return pl.ds(pl.multiple_of(first * DH, DH), count * DH)

    def scores_of(index, pack, s_ref, d_ref):
        head, t = index // 2, index % 2
        live = lax.broadcasted_iota(jnp.int32, (TILE, DH), 0) < lengths[t]
        first = head * GROUP + pack * PACK
        qs = [q_s[t, :, columns(first + j)] for j in range(PACK)]
        gs = [
            jnp.where(live, g_s[t, :, columns(first + j)], jnp.zeros((), BF16)) for j in range(PACK)
        ]
        q, g = jnp.concatenate(qs, axis=0), jnp.concatenate(gs, axis=0)

        def turn():
            for j in range(PACK):
                q_t[pack, :, j * TILE : (j + 1) * TILE] = qs[j].T
                g_t[pack, :, j * TILE : (j + 1) * TILE] = gs[j].T

        def root(of, ref, chunk, b):
            part = kv[chunk, b].reshape(R // SEGS, DH)
            ref[:, b * R // SEGS : (b + 1) * R // SEGS] = dot(of, part, NT)

        def branch(of, ref, start):
            ref[:, R:] = dot(of, branch_s[t, :, columns(start + head)], NT)

        pieces = []
        for of, ref, kind in ((q, s_ref, 0), (g, d_ref, 1)):
            pieces += [functools.partial(root, of, ref, 2 * head + kind, b) for b in range(SEGS)]
            pieces.append(functools.partial(branch, of, ref, kind * KVH))
        return pieces + [turn]

    def key_grads(index, pack, p_ref, is_first):
        part = R // SEGS

        def root(kind, ref, rows_t, b):
            cols = slice(b * part, (b + 1) * part)
            acc[kind, :, cols] = acc[kind, :, cols] + dot(rows_t[pack], ref[:, cols], NN)

        def branch(kind, ref, rows_t):
            term = dot(rows_t[pack], ref[:, R:], NN)
            branch_acc[kind] = term if is_first else branch_acc[kind] + term

        pieces = []
        for kind, ref, rows_t in ((1, p_ref, g_t), (0, ds_s[pack].at[index], q_t)):
            pieces += [functools.partial(root, kind, ref, rows_t, b) for b in range(SEGS)]
            pieces.append(functools.partial(branch, kind, ref, rows_t))
        return pieces

    def softmax_of(index, pack, s_ref, d_ref, p_ref):
        segment = segments[index % 2]
        ds_ref = ds_s[pack].at[index]
        count = PACK * TILE // ROWS

        def piece(i):
            if i + 2 * AHEAD < count:
                peaks((i + 2 * AHEAD) * ROWS, segment, s_ref, stats)
            if 0 <= i + AHEAD < count:
                exponentials((i + AHEAD) * ROWS, segment, s_ref, d_ref, stats)
            if i >= 0:
                weigh(i * ROWS, s_ref, d_ref, p_ref, ds_ref, stats)

        return [functools.partial(piece, i) for i in range(-2 * AHEAD, count)]

    def put_branch(index):
        head, t = index // 2, index % 2
        db_ref[t, :, columns(head)] = (branch_acc[0].T * SCALE).astype(BF16)
        db_ref[t, :, columns(KVH + head)] = branch_acc[1].T.astype(BF16)

    def put_root(head):
        shape = (NY, 2, NZ // 2, 2, 16, DH)
        for kind in range(2):
            rows = acc[kind].T
            rows = (rows * SCALE if kind == 0 else rows).astype(BF16).reshape(shape)
            for half in range(2):
                dpart[head, :, :, 2 * kind + half] = rows[:, :, :, half]
        acc[...] = jnp.zeros_like(acc)
        reduce_core(head)

    for chunk in range(CHUNKS):
        gather_z(chunk)
    for chunk in range(2):
        gather_y(chunk)
    acc[...] = jnp.zeros_like(acc)
    branch_acc[...] = jnp.zeros_like(branch_acc)
    q_t[1] = jnp.zeros_like(q_t[1])
    g_t[1] = jnp.zeros_like(g_t[1])
    pb[...] = jnp.zeros_like(pb)
    ds_b[2 * KVH] = jnp.zeros_like(pb)
    for chunk in range(2):
        gather_core(chunk)
    for chunk in range(2, 4):
        gather_y(chunk)
    b_copy.wait()
    q_copies[0].wait()
    g_copies[0].wait()
    gathered(0)
    gathered(1)
    for piece in scores_of(0, 0, sa, da):
        piece()

    def step(index, carry):
        head, t = index // 2, index % 2
        before = jnp.where(index == 0, 2 * KVH, index - 1)
        after = jnp.minimum(index + 1, 2 * KVH - 1)

        @pl.when(index == 0)
        def _():
            q_copies[1].wait()
            g_copies[1].wait()
            for chunk in range(4, CHUNKS):
                gather_y(chunk)

        interleaved(
            softmax_of(index, 0, sa, da, pa),
            key_grads(before, 1, pb, False) + scores_of(index, 1, sb, db),
        )

        @pl.when(index > 0)
        def _():
            put_branch(before)

        @pl.when(jnp.logical_and(t == 0, head >= 1))
        def _():
            put_root(head - 1)

        @pl.when(jnp.logical_and(t == 0, head < KVH - 1))
        def _():
            gather_core(2 * head + 2)
            gather_core(2 * head + 3)

        @pl.when(jnp.logical_and(t == 1, head < KVH - 1))
        def _():
            gathered(2 * head + 2)
            gathered(2 * head + 3)

        @pl.when(jnp.logical_and(t == 1, head >= 1))
        def _():
            reduce_plane(head - 1)

        @pl.when(jnp.logical_and(t == 1, head >= 2))
        def _():
            reduce_column(head - 2)

        interleaved(
            softmax_of(index, 1, sb, db, pb),
            key_grads(index, 0, pa, True) + scores_of(after, 0, sa, da),
        )

        @pl.when(jnp.logical_and(t == 0, head == KVH - 1))
        def _():
            share_sum(head - 3)

        return carry

    def query_grads(index, carry):
        head, t = index // 2, index % 2
        k_cols = pl.ds(pl.multiple_of(head * DH, DH), DH)
        for pack in range(2):
            rows = ds_s[pack].at[index]
            dq = dot(rows[:, :R], kv[2 * head].reshape(R, DH), NN)
            dq = dq + dot(rows[:, R:], branch_s[t, :, k_cols], NN)
            dq = (dq * SCALE).astype(BF16)
            for j in range(PACK):
                cols = columns(head * GROUP + pack * PACK + j)
                dq_ref[t, :, cols] = dq[j * TILE : (j + 1) * TILE]
        return carry

    last = KVH - 1
    lax.fori_loop(0, 2 * KVH, step, 0)
    for piece in key_grads(2 * KVH - 1, 1, pb, False):
        piece()
    put_root(last)
    put_branch(2 * KVH - 1)
    reduce_column(last - 1)
    lax.fori_loop(0, 1, query_grads, 0)
    reduce_plane(last)
    share_sum(last - 2)
    reduce_done(last - 3)
    lax.fori_loop(1, 5, query_grads, 0)
    share_sum(last - 1)
    reduce_column(last)
    reduce_done(last - 2)
    lax.fori_loop(5, 8, query_grads, 0)
    reduce_done(last - 1)
    share_sum(last)
    reduce_done(last)

    for _ in range(3):
        arrived(kv.at[:, 0, 0, 0], z_send)
        arrived(kv.at[:, 0, 0], y_send)
    arrived(kv.at[:, :, 0], c_send)
    arrived(r0, s0_send)
    arrived(r1, s1_send)
    arrived(r2, s2_send)
    arrived(r3.at[:, pl.ds(0, 3)], s3_send)


def local(query, grad_out, branch_kv, root_kv, lengths, segments):
    rows = R // 32
    anywhere = pl.BlockSpec(memory_space=pl.ANY)
    vmem = pl.BlockSpec(memory_space=pltpu.VMEM)
    smem = pl.BlockSpec(memory_space=pltpu.SMEM)
    dma = pltpu.SemaphoreType.DMA
    blocks = (CHUNKS, NY, 2, NZ // 2, rows, DH)
    half = (KVH, NY, NX, NZ // 2, 16, DH)
    return pl.pallas_call(
        kernel,
        out_shape=(
            jax.ShapeDtypeStruct(query.shape, BF16),
            jax.ShapeDtypeStruct(branch_kv.shape, BF16),
            jax.ShapeDtypeStruct(root_kv.shape, F32),
        ),
        in_specs=[smem, smem, anywhere, anywhere, anywhere, vmem],
        out_specs=(vmem, vmem, vmem),
        scratch_shapes=[
            pltpu.VMEM(query.shape, BF16),
            pltpu.VMEM(query.shape, BF16),
            pltpu.VMEM(branch_kv.shape, BF16),
            pltpu.VMEM(blocks, BF16),
            *[pltpu.VMEM((PACK * TILE, R + TILE), F32)] * 4,
            *[pltpu.VMEM((PACK * TILE, R + TILE), BF16)] * 2,
            *[pltpu.VMEM((2 * KVH + 1, PACK * TILE, R + TILE), BF16)] * 2,
            pltpu.VMEM((2, DH, PACK * TILE), BF16),
            pltpu.VMEM((2, DH, PACK * TILE), BF16),
            pltpu.VMEM((2, DH, R), F32),
            pltpu.VMEM((2, DH, TILE), F32),
            pltpu.VMEM((3, PACK * TILE, DH), F32),
            pltpu.VMEM((KVH, NY, 2, NX, NZ // 2, 16, DH), BF16),
            pltpu.VMEM(half, BF16),
            pltpu.VMEM(half, BF16),
            pltpu.VMEM((KVH, NX * NY - 1, NZ // 2, 16, DH), BF16),
            pltpu.VMEM((KVH, NZ // 2, 16, DH), BF16),
            pltpu.VMEM((KVH, NZ - 1, 16, DH), BF16),
            pltpu.VMEM((KVH, 16, DH), F32),
            pltpu.VMEM((KVH, NX, 16, DH), F32),
            dma((5,)),
            dma,
            dma((CHUNKS,)),
            dma,
            dma((CHUNKS,)),
            dma,
            dma((CHUNKS,)),
            dma,
            dma((KVH,)),
            dma,
            dma((KVH,)),
            dma,
            dma((KVH,)),
            dma,
            dma((KVH,)),
        ],
        compiler_params=pltpu.CompilerParams(
            collective_id=0, has_side_effects=True, vmem_limit_bytes=48 << 20
        ),
    )(lengths, segments, query, grad_out, branch_kv, root_kv)


def solution(mesh):
    placed = (
        P(("grp", "dev"), None, None),
        P(("grp", "dev"), None, None),
        P(("grp", "dev"), None, None),
        P("dev", None),
        P(("grp", "dev")),
        P(("grp", "dev")),
    )
    return jax.shard_map(
        local,
        mesh=mesh,
        in_specs=placed,
        out_specs=(P(("grp", "dev"), None, None), P(("grp", "dev"), None, None), P("dev", None)),
        check_vma=False,
    )
```

time: 104 us -> 80.6 us (0.77); the launches traced: 103 us -> 80.4 us
  Pallas kernels: 97.4 us -> 72.2 us
  local copies, waits for them, and re-layouts: 4.65 us -> 7.54 us
    pallas_call x1, Pallas kernels: 97.4 us -> 72.2 us  [local(): pl.pallas_call(kernel, out_shape=(jax.ShapeDtypeStruct(query.shape, BF16)...]
    unnamed x7 -> x13, local copies, waits for them, and re-layouts: 4.65 us -> 7.54 us
where the time goes in v2:
time: 80.6 us; the launch traced here: 80.4 us
  Pallas kernels  72.2 us (90%)
  local copies, waits for them, and re-layouts  7.54 us (9%)
    pallas_call x1, Pallas kernels, local(): pl.pallas_call(kernel, out_shape=(jax.ShapeDtypeStruct(query.shape, BF16)...  72.2 us
    unnamed x13, local copies, waits for them, and re-layouts  7.54 us

profile of v2, /device:TPU:8, one launch (start us, length us, event | category | flops | bytes accessed | tf_op | source)
XLA Modules:
  0.0 80.4 jit_solution(4860166170011721746)
XLA Ops:
  0.6 0.0 copy-start
  0.6 1.6 %copy-done = bf16[2,128,4096]{2,1,0:T(8,128)(2,1)S(1)} copy-done((bf16[2,128,4096]{2,1,0:T(8,128)(2,1)S(1)}, bf16[2,128,4096]{2,1,0:T(8,128)(2,1)}, u32[]{:S(2)}) %copy-start) | copy-done | bytes 2097176
  2.2 0.0 copy-start.1
  2.2 1.0 %copy-done.1 = bf16[2,128,1024]{2,1,0:T(8,128)(2,1)S(1)} copy-done((bf16[2,128,1024]{2,1,0:T(8,128)(2,1)S(1)}, bf16[2,128,1024]{2,1,0:T(8,128)(2,1)}, u32[]{:S(2)}) %copy-start.1) | copy-done | bytes 524312
  3.3 0.0 copy-start.2
  3.3 0.8 %copy-done.2 = bf16[32,1024]{1,0:T(8,128)(2,1)S(1)} copy-done((bf16[32,1024]{1,0:T(8,128)(2,1)S(1)}, bf16[32,1024]{1,0:T(8,128)(2,1)}, u32[]{:S(2)}) %copy-start.2) | copy-done | bytes 65560
  4.1 0.0 copy-start.3
  4.1 0.7 copy-done.3
  4.8 0.0 copy-start.4
  4.8 0.7 copy-done.4
  5.4 72.2 %shard_map.85 = (bf16[2,128,4096]{2,1,0:T(8,128)(2,1)S(1)}, bf16[2,128,1024]{2,1,0:T(8,128)(2,1)S(1)}, f32[32,1024]{1,0:T(8,128)S(1)}) custom-call(s32[2]{0:T(128)S(1)} %copy-done.3, s32[2]{0:T(128)S(1)} %copy-done.4, bf16[2,128,4096]{2,1,0:T(8,128)(2,1)S(1)} %copy-done, bf16[2,128,4096]{2,1,0:T(8,128)(2,1)} %g_hbm.1, bf16[2,128,1024]{2,1,0:T(8,128)(2,1)S(1)} %copy-done.1, ...), custom_call_target="tpu_custom_call" | custom-call | tf_op jit(solution)/shard_map/pallas_call | solution.py:470
  77.6 1.3 %copy.12 = bf16[2,128,4096]{2,1,0:T(8,128)(2,1)} copy(bf16[2,128,4096]{2,1,0:T(8,128)(2,1)S(1)} %get-tuple-element.6) | data formatting | bytes 4194304
  79.0 0.8 copy.13
  79.8 0.7 copy.14
Async XLA Ops:
  0.6 1.6 %copy-start = (bf16[2,128,4096]{2,1,0:T(8,128)(2,1)S(1)}, bf16[2,128,4096]{2,1,0:T(8,128)(2,1)}, u32[]{:S(2)}) copy-start(bf16[2,128,4096]{2,1,0:T(8,128)(2,1)} %q_hbm.1) | copy-start | bytes 6291460
  2.2 1.0 %copy-start.1 = (bf16[2,128,1024]{2,1,0:T(8,128)(2,1)S(1)}, bf16[2,128,1024]{2,1,0:T(8,128)(2,1)}, u32[]{:S(2)}) copy-start(bf16[2,128,1024]{2,1,0:T(8,128)(2,1)} %branch_hbm.1) | copy-start | bytes 1572868
  3.3 0.8 %copy-start.2 = (bf16[32,1024]{1,0:T(8,128)(2,1)S(1)}, bf16[32,1024]{1,0:T(8,128)(2,1)}, u32[]{:S(2)}) copy-start(bf16[32,1024]{1,0:T(8,128)(2,1)} %root_ref.1) | copy-start | bytes 196612
  4.1 0.7 copy-start.3
  4.8 0.7 copy-start.4

commit v3 on v2

--- a/solution.py
+++ b/solution.py
@@ -104,18 +104,21 @@
 
 
 def kernel(
-    lengths,
-    segments,
+    lengths_hbm,
+    segments_hbm,
     q_hbm,
     g_hbm,
     branch_hbm,
-    root_ref,
+    root_hbm,
     dq_ref,
     db_ref,
     out_ref,
+    lengths,
+    segments,
     q_s,
     g_s,
     branch_s,
+    root_ref,
     kv,
     sa,
     sb,
@@ -168,7 +171,8 @@
 
     away = 2 * z_lo - 1
     z_dests = [at(x, y, ring_z(away * k), c) for k in (1, 2, 3)]
-    y_dests = [at(x, (y + k) % NY, z, c) for k in (1, 2, 3)]
+    y_dests = [at(x, (y + k) % NY, z, c) for k in (1, 3)]
+    y_from = [(y + k) % NY for k in (3, 1)]
     other_core = at(x, y, z, 1 - c)
     plane = [((x + k // NY) % NX, (y + k % NY) % NY) for k in range(1, NX * NY)]
     column = [(z + k) % NZ for k in range(1, NZ)]
@@ -177,7 +181,12 @@
     q_copies = [pltpu.make_async_copy(q_hbm.at[t], q_s.at[t], in_sem.at[t]) for t in range(2)]
     g_copies = [pltpu.make_async_copy(g_hbm.at[t], g_s.at[t], in_sem.at[2 + t]) for t in range(2)]
     b_copy = pltpu.make_async_copy(branch_hbm, branch_s, in_sem.at[4])
-    for copy in (b_copy, q_copies[0], g_copies[0], q_copies[1], g_copies[1]):
+    small = (
+        pltpu.make_async_copy(lengths_hbm, lengths, in_sem.at[5]),
+        pltpu.make_async_copy(segments_hbm, segments, in_sem.at[6]),
+        pltpu.make_async_copy(root_hbm, root_ref, in_sem.at[7]),
+    )
+    for copy in (*small[::-1], b_copy, q_copies[0], g_copies[0], q_copies[1], g_copies[1]):
         copy.start()
 
     barrier = pltpu.get_barrier_semaphore()
@@ -213,22 +222,38 @@
         for device in z_dests:
             remote(src, dst, z_send, z_recv.at[chunk], device).start()
 
+    def to_core(chunk, py):
+        block = kv.at[chunk, py, c]
+        remote(block, block, c_send, c_recv.at[chunk], other_core).start()
+
     def gather_y(chunk):
         block = kv.at[chunk, y, c]
         arrived(block, z_recv.at[chunk])
-        for device in y_dests:
-            remote(block, block, y_send, y_recv.at[chunk], device).start()
+        for side in range(2):
+            remote(block, block, y_send, y_recv.at[chunk, side], y_dests[side]).start()
+        to_core(chunk, y)
+
+    def relay_y(chunk):
+        for side in range(2):
+            py = y_from[side]
+            arrived(kv.at[chunk, py, c], y_recv.at[chunk, side])
+            block = kv.at[chunk, py, c, pl.ds(2 * side, 2)]
+            remote(block, block, y_send, y_recv.at[chunk, 2], y_dests[side]).start()
+        for side in range(2):
+            to_core(chunk, y_from[side])
 
     def gather_core(chunk):
-        arrived(kv.at[chunk, pl.ds(0, 3), c], y_recv.at[chunk])
-        block = kv.at[chunk, :, c]
-        remote(block, block, c_send, c_recv.at[chunk], other_core).start()
+        far = (y + 2) % NY
+        arrived(kv.at[chunk, far, c], y_recv.at[chunk, 2])
+        to_core(chunk, far)
 
     def gathered(chunk):
         arrived(kv.at[chunk, :, 1 - c], c_recv.at[chunk])
 
-    def reduce_core(head):
-        remote(dpart.at[head, :, 1 - c], r0.at[head], s0_send, s0_recv.at[head], other_core).start()
+    def reduce_core(head, kind):
+        both = pl.ds(2 * kind, 2)
+        src, dst = dpart.at[head, :, 1 - c, both], r0.at[head, :, both]
+        remote(src, dst, s0_send, s0_recv.at[head], other_core).start()
 
     def reduce_plane(head):
         arrived(r0.at[head], s0_recv.at[head])
@@ -332,14 +357,16 @@
 
     def put_root(head):
         shape = (NY, 2, NZ // 2, 2, 16, DH)
-        for kind in range(2):
+        for kind in (1, 0):
             rows = acc[kind].T
             rows = (rows * SCALE if kind == 0 else rows).astype(BF16).reshape(shape)
             for half in range(2):
                 dpart[head, :, :, 2 * kind + half] = rows[:, :, :, half]
+            reduce_core(head, kind)
         acc[...] = jnp.zeros_like(acc)
-        reduce_core(head)
-
+
+    for copy in small:
+        copy.wait()
     for chunk in range(CHUNKS):
         gather_z(chunk)
     for chunk in range(2):
@@ -351,9 +378,11 @@
     pb[...] = jnp.zeros_like(pb)
     ds_b[2 * KVH] = jnp.zeros_like(pb)
     for chunk in range(2):
+        relay_y(chunk)
+    for chunk in range(2, CHUNKS):
+        gather_y(chunk)
+    for chunk in range(2):
         gather_core(chunk)
-    for chunk in range(2, 4):
-        gather_y(chunk)
     b_copy.wait()
     q_copies[0].wait()
     g_copies[0].wait()
@@ -362,17 +391,20 @@
     for piece in scores_of(0, 0, sa, da):
         piece()
 
-    def step(index, carry):
+    def step(index, carry, final=False):
         head, t = index // 2, index % 2
         before = jnp.where(index == 0, 2 * KVH, index - 1)
-        after = jnp.minimum(index + 1, 2 * KVH - 1)
+        after = index + 1
 
         @pl.when(index == 0)
         def _():
             q_copies[1].wait()
             g_copies[1].wait()
-            for chunk in range(4, CHUNKS):
-                gather_y(chunk)
+
+        @pl.when(jnp.logical_and(t == 0, head < KVH - 1))
+        def _():
+            relay_y(2 * head + 2)
+            relay_y(2 * head + 3)
 
         interleaved(
             softmax_of(index, 0, sa, da, pa),
@@ -407,7 +439,7 @@
 
         interleaved(
             softmax_of(index, 1, sb, db, pb),
-            key_grads(index, 0, pa, True) + scores_of(after, 0, sa, da),
+            key_grads(index, 0, pa, True) + ([] if final else scores_of(after, 0, sa, da)),
         )
 
         @pl.when(jnp.logical_and(t == 0, head == KVH - 1))
@@ -430,7 +462,8 @@
         return carry
 
     last = KVH - 1
-    lax.fori_loop(0, 2 * KVH, step, 0)
+    lax.fori_loop(0, 2 * KVH - 1, step, 0)
+    step(jnp.int32(2 * KVH - 1), 0, final=True)
     for piece in key_grads(2 * KVH - 1, 1, pb, False):
         piece()
     put_root(last)
@@ -461,9 +494,8 @@
 
 def local(query, grad_out, branch_kv, root_kv, lengths, segments):
     rows = R // 32
-    anywhere = pl.BlockSpec(memory_space=pl.ANY)
+    hbm = pl.BlockSpec(memory_space=pltpu.HBM)
     vmem = pl.BlockSpec(memory_space=pltpu.VMEM)
-    smem = pl.BlockSpec(memory_space=pltpu.SMEM)
     dma = pltpu.SemaphoreType.DMA
     blocks = (CHUNKS, NY, 2, NZ // 2, rows, DH)
     half = (KVH, NY, NX, NZ // 2, 16, DH)
@@ -474,12 +506,15 @@
             jax.ShapeDtypeStruct(branch_kv.shape, BF16),
             jax.ShapeDtypeStruct(root_kv.shape, F32),
         ),
-        in_specs=[smem, smem, anywhere, anywhere, anywhere, vmem],
+        in_specs=[hbm] * 6,
         out_specs=(vmem, vmem, vmem),
         scratch_shapes=[
+            pltpu.SMEM(lengths.shape, jnp.int32),
+            pltpu.SMEM(segments.shape, jnp.int32),
             pltpu.VMEM(query.shape, BF16),
             pltpu.VMEM(query.shape, BF16),
             pltpu.VMEM(branch_kv.shape, BF16),
+            pltpu.VMEM(root_kv.shape, BF16),
             pltpu.VMEM(blocks, BF16),
             *[pltpu.VMEM((PACK * TILE, R + TILE), F32)] * 4,
             *[pltpu.VMEM((PACK * TILE, R + TILE), BF16)] * 2,
@@ -497,11 +532,11 @@
             pltpu.VMEM((KVH, NZ - 1, 16, DH), BF16),
             pltpu.VMEM((KVH, 16, DH), F32),
             pltpu.VMEM((KVH, NX, 16, DH), F32),
-            dma((5,)),
+            dma((8,)),
             dma,
             dma((CHUNKS,)),
             dma,
-            dma((CHUNKS,)),
+            dma((CHUNKS, 3)),
             dma,
             dma((CHUNKS,)),
             dma,
@@ -514,9 +549,9 @@
             dma((KVH,)),
         ],
         compiler_params=pltpu.CompilerParams(
-            collective_id=0, has_side_effects=True, vmem_limit_bytes=48 << 20
+            collective_id=0, has_side_effects=True, vmem_limit_bytes=49 << 20
         ),
-    )(lengths, segments, query, grad_out, branch_kv, root_kv)
+    )(*[pltpu.with_memory_space_constraint(a, pltpu.HBM) for a in (lengths, segments, query, grad_out, branch_kv, root_kv)])
 
 
 def solution(mesh):

time: 80.6 us -> 82.3 us (1.021)
  Pallas kernels: 72.2 us -> 78.2 us
  local copies, waits for them, and re-layouts: 7.54 us -> 2.77 us
    pallas_call x1, Pallas kernels: 72.2 us -> 78.2 us  [local(): pl.pallas_call(kernel, out_shape=(jax.ShapeDtypeStruct(query.shape, BF16)...]
    unnamed x13 -> x3, local copies, waits for them, and re-layouts: 7.54 us -> 2.77 us
where the time goes in v3:
time: 82.3 us; the launch traced here: 81.6 us
  Pallas kernels  78.2 us (95%)
  local copies, waits for them, and re-layouts  2.77 us (3%)
    pallas_call x1, Pallas kernels, local(): pl.pallas_call(kernel, out_shape=(jax.ShapeDtypeStruct(query.shape, BF16)...  78.2 us
    unnamed x3, local copies, waits for them, and re-layouts  2.77 us

profile of v3, /device:TPU:8, one launch (start us, length us, event | category | flops | bytes accessed | tf_op | source)
XLA Modules:
  0.0 81.6 jit_solution(10384534014040294050)
XLA Ops:
  0.6 78.2 %shard_map.85 = (bf16[2,128,4096]{2,1,0:T(8,128)(2,1)S(1)}, bf16[2,128,1024]{2,1,0:T(8,128)(2,1)S(1)}, f32[32,1024]{1,0:T(8,128)S(1)}) custom-call(s32[2]{0:T(128)} %lengths_hbm.1, s32[2]{0:T(128)} %segments_hbm.1, bf16[2,128,4096]{2,1,0:T(8,128)(2,1)} %q_hbm.1, bf16[2,128,4096]{2,1,0:T(8,128)(2,1)} %g_hbm.1, bf16[2,128,1024]{2,1,0:T(8,128)(2,1)} %branch_hbm.1, ...), custom_call_target="tpu_custom_call" | custom-call | tf_op jit(solution)/shard_map/pallas_call | solution.py:502
  78.8 1.3 %copy.12 = bf16[2,128,4096]{2,1,0:T(8,128)(2,1)} copy(bf16[2,128,4096]{2,1,0:T(8,128)(2,1)S(1)} %get-tuple-element.6) | data formatting | bytes 4194304
  80.1 0.8 copy.13
  80.9 0.7 copy.14

commit v4 on v3

--- a/solution.py
+++ b/solution.py
@@ -171,8 +171,7 @@
 
     away = 2 * z_lo - 1
     z_dests = [at(x, y, ring_z(away * k), c) for k in (1, 2, 3)]
-    y_dests = [at(x, (y + k) % NY, z, c) for k in (1, 3)]
-    y_from = [(y + k) % NY for k in (3, 1)]
+    y_dests = [at(x, (y + k) % NY, z, c) for k in (1, 2, 3)]
     other_core = at(x, y, z, 1 - c)
     plane = [((x + k // NY) % NX, (y + k % NY) % NY) for k in range(1, NX * NY)]
     column = [(z + k) % NZ for k in range(1, NZ)]
@@ -222,30 +221,16 @@
         for device in z_dests:
             remote(src, dst, z_send, z_recv.at[chunk], device).start()
 
-    def to_core(chunk, py):
-        block = kv.at[chunk, py, c]
-        remote(block, block, c_send, c_recv.at[chunk], other_core).start()
-
     def gather_y(chunk):
         block = kv.at[chunk, y, c]
         arrived(block, z_recv.at[chunk])
-        for side in range(2):
-            remote(block, block, y_send, y_recv.at[chunk, side], y_dests[side]).start()
-        to_core(chunk, y)
-
-    def relay_y(chunk):
-        for side in range(2):
-            py = y_from[side]
-            arrived(kv.at[chunk, py, c], y_recv.at[chunk, side])
-            block = kv.at[chunk, py, c, pl.ds(2 * side, 2)]
-            remote(block, block, y_send, y_recv.at[chunk, 2], y_dests[side]).start()
-        for side in range(2):
-            to_core(chunk, y_from[side])
+        for device in y_dests:
+            remote(block, block, y_send, y_recv.at[chunk], device).start()
 
     def gather_core(chunk):
-        far = (y + 2) % NY
-        arrived(kv.at[chunk, far, c], y_recv.at[chunk, 2])
-        to_core(chunk, far)
+        arrived(kv.at[chunk, pl.ds(0, 3), c], y_recv.at[chunk])
+        block = kv.at[chunk, :, c]
+        remote(block, block, c_send, c_recv.at[chunk], other_core).start()
 
     def gathered(chunk):
         arrived(kv.at[chunk, :, 1 - c], c_recv.at[chunk])
@@ -378,11 +363,9 @@
     pb[...] = jnp.zeros_like(pb)
     ds_b[2 * KVH] = jnp.zeros_like(pb)
     for chunk in range(2):
-        relay_y(chunk)
-    for chunk in range(2, CHUNKS):
+        gather_core(chunk)
+    for chunk in range(2, 4):
         gather_y(chunk)
-    for chunk in range(2):
-        gather_core(chunk)
     b_copy.wait()
     q_copies[0].wait()
     g_copies[0].wait()
@@ -400,11 +383,8 @@
         def _():
             q_copies[1].wait()
             g_copies[1].wait()
-
-        @pl.when(jnp.logical_and(t == 0, head < KVH - 1))
-        def _():
-            relay_y(2 * head + 2)
-            relay_y(2 * head + 3)
+            for chunk in range(4, CHUNKS):
+                gather_y(chunk)
 
         interleaved(
             softmax_of(index, 0, sa, da, pa),
@@ -536,7 +516,7 @@
             dma,
             dma((CHUNKS,)),
             dma,
-            dma((CHUNKS, 3)),
+            dma((CHUNKS,)),
             dma,
             dma((CHUNKS,)),
             dma,

time: 82.3 us -> 76 us (0.923)
  Pallas kernels: 78.2 us -> 72.5 us
    pallas_call x1, Pallas kernels: 78.2 us -> 72.5 us  [local(): pl.pallas_call(kernel, out_shape=(jax.ShapeDtypeStruct(query.shape, BF16)...]
where the time goes in v4:
time: 76 us; the launch traced here: 75.9 us
  Pallas kernels  72.5 us (95%)
  local copies, waits for them, and re-layouts  2.77 us (4%)
    pallas_call x1, Pallas kernels, local(): pl.pallas_call(kernel, out_shape=(jax.ShapeDtypeStruct(query.shape, BF16)...  72.5 us
    unnamed x3, local copies, waits for them, and re-layouts  2.77 us

profile of v4, /device:TPU:8, one launch (start us, length us, event | category | flops | bytes accessed | tf_op | source)
XLA Modules:
  0.0 75.9 jit_solution(6161535667351661620)
XLA Ops:
  0.6 72.5 %shard_map.85 = (bf16[2,128,4096]{2,1,0:T(8,128)(2,1)S(1)}, bf16[2,128,1024]{2,1,0:T(8,128)(2,1)S(1)}, f32[32,1024]{1,0:T(8,128)S(1)}) custom-call(s32[2]{0:T(128)} %lengths_hbm.1, s32[2]{0:T(128)} %segments_hbm.1, bf16[2,128,4096]{2,1,0:T(8,128)(2,1)} %q_hbm.1, bf16[2,128,4096]{2,1,0:T(8,128)(2,1)} %g_hbm.1, bf16[2,128,1024]{2,1,0:T(8,128)(2,1)} %branch_hbm.1, ...), custom_call_target="tpu_custom_call" | custom-call | tf_op jit(solution)/shard_map/pallas_call | solution.py:482
  73.1 1.3 %copy.12 = bf16[2,128,4096]{2,1,0:T(8,128)(2,1)} copy(bf16[2,128,4096]{2,1,0:T(8,128)(2,1)S(1)} %get-tuple-element.6) | data formatting | bytes 4194304
  74.5 0.8 %copy.13 = bf16[2,128,1024]{2,1,0:T(8,128)(2,1)} copy(bf16[2,128,1024]{2,1,0:T(8,128)(2,1)S(1)} %get-tuple-element.7) | data formatting | bytes 1048576
  75.2 0.7 copy.14

commit v5 on v4

--- a/solution.py
+++ b/solution.py
@@ -170,12 +170,14 @@
         return (z + offset + NZ) % NZ
 
     away = 2 * z_lo - 1
-    z_dests = [at(x, y, ring_z(away * k), c) for k in (1, 2, 3)]
-    y_dests = [at(x, (y + k) % NY, z, c) for k in (1, 2, 3)]
+    z_dests = [at(x, y, ring_z(away * k), c) for k in (3, 2, 1)]
+    y_dests = [at(x, (y + k) % NY, z, c) for k in (2, 1, 3)]
     other_core = at(x, y, z, 1 - c)
-    plane = [((x + k // NY) % NX, (y + k % NY) % NY) for k in range(1, NX * NY)]
-    column = [(z + k) % NZ for k in range(1, NZ)]
-    x_dests = [at((x + k) % NX, y, z, c) for k in (1, 2, 3)]
+    hops = (0, 1, 2, 1)
+    farthest_first = sorted(range(1, NX * NY), key=lambda k: -hops[k // NY] - hops[k % NY])
+    plane = [((x + k // NY) % NX, (y + k % NY) % NY) for k in farthest_first]
+    column = [(z + k) % NZ for k in (4, 3, 5, 2, 6, 1, 7)]
+    x_dests = [at((x + k) % NX, y, z, c) for k in (2, 1, 3)]
 
     q_copies = [pltpu.make_async_copy(q_hbm.at[t], q_s.at[t], in_sem.at[t]) for t in range(2)]
     g_copies = [pltpu.make_async_copy(g_hbm.at[t], g_s.at[t], in_sem.at[2 + t]) for t in range(2)]
@@ -369,9 +371,14 @@
     b_copy.wait()
     q_copies[0].wait()
     g_copies[0].wait()
+    pieces = scores_of(0, 0, sa, da)
+    for piece in pieces[SEGS : SEGS + 1] + pieces[2 * SEGS + 1 :]:
+        piece()
     gathered(0)
+    for piece in pieces[:SEGS]:
+        piece()
     gathered(1)
-    for piece in scores_of(0, 0, sa, da):
+    for piece in pieces[SEGS + 1 : 2 * SEGS + 1]:
         piece()
 
     def step(index, carry, final=False):

time: 76 us -> 73.8 us (0.971)
  Pallas kernels: 72.5 us -> 70.1 us
    pallas_call x1, Pallas kernels: 72.5 us -> 70.1 us  [local(): pl.pallas_call(kernel, out_shape=(jax.ShapeDtypeStruct(query.shape, BF16)...]
where the time goes in v5:
time: 73.8 us; the launch traced here: 73.5 us
  Pallas kernels  70.1 us (95%)
  local copies, waits for them, and re-layouts  2.77 us (4%)
    pallas_call x1, Pallas kernels, local(): pl.pallas_call(kernel, out_shape=(jax.ShapeDtypeStruct(query.shape, BF16)...  70.1 us
    unnamed x3, local copies, waits for them, and re-layouts  2.77 us

profile of v5, /device:TPU:8, one launch (start us, length us, event | category | flops | bytes accessed | tf_op | source)
XLA Modules:
  0.0 73.5 jit_solution(499092570696214405)
XLA Ops:
  0.6 70.1 %shard_map.85 = (bf16[2,128,4096]{2,1,0:T(8,128)(2,1)S(1)}, bf16[2,128,1024]{2,1,0:T(8,128)(2,1)S(1)}, f32[32,1024]{1,0:T(8,128)S(1)}) custom-call(s32[2]{0:T(128)} %lengths_hbm.1, s32[2]{0:T(128)} %segments_hbm.1, bf16[2,128,4096]{2,1,0:T(8,128)(2,1)} %q_hbm.1, bf16[2,128,4096]{2,1,0:T(8,128)(2,1)} %g_hbm.1, bf16[2,128,1024]{2,1,0:T(8,128)(2,1)} %branch_hbm.1, ...), custom_call_target="tpu_custom_call" | custom-call | tf_op jit(solution)/shard_map/pallas_call | solution.py:489
  70.7 1.3 %copy.12 = bf16[2,128,4096]{2,1,0:T(8,128)(2,1)} copy(bf16[2,128,4096]{2,1,0:T(8,128)(2,1)S(1)} %get-tuple-element.6) | data formatting | bytes 4194304
  72.0 0.8 %copy.13 = bf16[2,128,1024]{2,1,0:T(8,128)(2,1)} copy(bf16[2,128,1024]{2,1,0:T(8,128)(2,1)S(1)} %get-tuple-element.7) | data formatting | bytes 1048576
  72.8 0.7 copy.14
